TPU v7x, 32 devices: a whole 2x2x4 slice. The times are simulated.
32 devices in a mesh: row: 8 (over y, x, core), col: 4 (over z).
Axes of the slice: x: 2, y: 2, z: 4, core: 2. Of those that a mesh axis runs over, the one named last changes fastest.
Arguments:
- key_rows: float32 [128, 20480], P('col', 'row'), may hold values from -0.0390625 to 0.0390625
- targets: float32 [128, 7168], P(None, 'col'), may hold values from -24 to 24
- weight: float32 [20480, 7168], P('row', 'col'), may hold values from -6 to 6
- covariance: float32 [20480, 20480], P('row', 'col'), may hold values from -3 to 24, as said below
Outputs:
- increment: float32 [20480, 7168], P('row', 'col')
Inputs may be any that keep to these rules, and one draw needn't show every extreme that they name: covariance is symmetric and positive definite.
All inputs are finite; a program needn't handle non-finite values.
Results may differ from a plain program's by a relative error of at most 0.0003.
Values sent between devices are 32-bit elements; how exact they have to be, the bound alone decides.
No kernel may reach another device: no remote copies, remote signals or barrier semaphores. Data moves between devices by JAX's collectives and lax.ppermute only.
A program may use at most 192 MiB of HBM per device.

v0:
```python
import jax
import jax.numpy as jnp
from jax import lax
from jax.sharding import PartitionSpec as P


def spread(value, axis, root):
    mine = lax.axis_index(axis) == root
    return lax.psum(jnp.where(mine, value, jnp.zeros_like(value)), axis)


def precise(left, right):
    return jnp.dot(left, right, precision=lax.Precision.HIGHEST, preferred_element_type=jnp.float32)


def transposed_product(left, right):
    return lax.dot_general(
        left,
        right,
        (((0,), (0,)), ((), ())),
        precision=lax.Precision.HIGHEST,
        preferred_element_type=jnp.float32,
    )


def definite_solve(matrix, right_side):
    factor = jnp.linalg.cholesky(0.5 * (matrix + matrix.T))
    return jax.scipy.linalg.cho_solve((factor, True), right_side)


def fetch_panel(local_rows):
    blocks_per = lax.axis_size("row") // lax.axis_size("col")
    col_index = lax.axis_index("col")
    pieces = []
    for part_index in range(blocks_per):
        pieces.append(spread(local_rows, "row", col_index * blocks_per + part_index))
    return jnp.concatenate(pieces, axis=0)


def covariance_rows(covariance, local_rows):
    panel_rows = fetch_panel(local_rows)
    return lax.psum(precise(covariance, panel_rows), "col")


def body(key_rows, targets, weight, covariance):
    all_keys = lax.all_gather(key_rows, "col", axis=0, tiled=True)
    basis_panel = all_keys.T
    fitted, gram_keys = lax.psum((precise(all_keys, weight), precise(all_keys, basis_panel)), "row")
    residual = targets - fitted
    image_one = covariance_rows(covariance, basis_panel) + precise(basis_panel, gram_keys)
    curvature, square = lax.psum(
        (transposed_product(basis_panel, image_one), transposed_product(image_one, image_one)),
        "row",
    )
    alpha_one = definite_solve(curvature, gram_keys)
    residual_next = basis_panel - precise(image_one, alpha_one)
    norm_next = transposed_product(alpha_one, precise(square, alpha_one)) - gram_keys
    beta_one = definite_solve(gram_keys, norm_next)
    direction = residual_next + precise(basis_panel, beta_one)
    key_part = precise(all_keys, direction)
    cov_direction = covariance_rows(covariance, direction)
    key_direction, curve_part = lax.psum(
        (key_part, transposed_product(direction, cov_direction)), "row"
    )
    curvature_two = curve_part + transposed_product(key_direction, key_direction)
    alpha_two = definite_solve(curvature_two, norm_next)
    solved = precise(basis_panel, alpha_one) + precise(direction, alpha_two)
    return precise(solved, residual)


def solution(mesh):
    placed = (P("col", "row"), P(None, "col"), P("row", "col"), P("row", "col"))
    return jax.shard_map(
        body, mesh=mesh, in_specs=placed, out_specs=P("row", "col"), check_vma=False
    )
```

profile of v0, /device:TPU:0, one launch (start us, length us, event | category | flops | bytes accessed | tf_op | source)
XLA Modules:
  0.0 627.3 jit_solution(12307424067801751636)
XLA Ops:
  7.3 37.0 %all-gather.2.cloned.1.call-done = f32[128,2560]{1,0:T(8,128)} async-done(((f32[32,2560]{1,0:T(8,128)}), f32[128,2560]{1,0:T(8,128)}) %all-gather.2.cloned.1.call-update) | async-done | bytes 1310736 | tf_op jit(solution)/shard_map/all_gather | solution.py:46
  44.4 1.7 copy.14
  46.1 1.7 bitcast_select_fusion.1
  48.3 1.8 fusion.33
  50.2 64.8 %all-reduce.21.cloned.1.call-done = (f32[128,128]{1,0:T(8,128)}, f32[2560,128]{1,0:T(8,128)}, f32[2560,128]{1,0:T(8,128)}) async-done(((f32[128,128]{1,0:T(8,128)}, f32[2560,128]{1,0:T(8,128)}, f32[2560,128]{1,0:T(8,128)}), (f32[128,128]{1,0:T(8,128)}, f32[2560,128]{1,0:T(8,128)}, f32[2560,128]{1,0:T(8,128)})) %all-reduce.21.cloned.1.call-update) | async-done | bytes 2686992 | tf_op jit(solution)/shard_map/psum | solution.py:48
  115.1 60.9 %convolution_bitcast_fusion.4 = f32[2560,128]{0,1:T(8,128)} fusion(f32[2560,5120]{1,0:T(8,128)} %param.10, f32[2560,128]{1,0:T(8,128)} %get-tuple-element.15, f32[2560,128]{1,0:T(8,128)} %get-tuple-element.16), kind=kOutput, calls=%fused_computation.8 | convolution fusion | flops 20133314560 | bytes 56360960 | tf_op jit(solution)/shard_map/dot_general | solution.py:13
  177.1 11.7 %cholesky.70 = f32[128,128]{1,0:T(8,128)S(1)} custom-call(f32[128,128]{1,0:T(8,128)S(1)} %fusion.23), custom_call_target="Cholesky" | custom-call | tf_op jit(solution)/shard_map/jit(cholesky)/cholesky | solution.py:27
  189.5 46.5 %all-reduce.11.cloned.1.call-done = f32[2560,128]{0,1:T(8,128)} async-done(((f32[2560,128]{0,1:T(8,128)}), f32[2560,128]{0,1:T(8,128)}) %all-reduce.11.cloned.1.call-update) | async-done | bytes 1310736 | tf_op jit(solution)/shard_map/psum | solution.py:42
  236.0 2.6 fusion.1
  238.6 1.8 fusion.34
  240.4 1.8 convolution_bitcast_fusion.6
  243.4 9.8 %custom-call.10 = f32[1,128,128]{1,2,0:T(8,128)S(1)} custom-call(f32[1,128,128]{2,1,0:T(8,128)S(1)} %fusion.11), custom_call_target="InvertDiagBlocksLowerTriangular" | custom-call | tf_op jit(solution)/shard_map/jit(_cho_solve)/triangular_solve | solution.py:28
  253.2 42.0 %all-reduce.19.cloned.1.call-done = (f32[128,128]{1,0:T(8,128)}, f32[128,128]{1,0:T(8,128)}) async-done(((f32[128,128]{1,0:T(8,128)}, f32[128,128]{1,0:T(8,128)}), (f32[128,128]{1,0:T(8,128)}, f32[128,128]{1,0:T(8,128)})) %all-reduce.19.cloned.1.call-update) | async-done | bytes 131088 | tf_op jit(solution)/shard_map/psum | solution.py:51
  295.2 0.9 copy.16
  297.1 11.7 %cholesky.59 = f32[128,128]{1,0:T(8,128)S(1)} custom-call(f32[128,128]{1,0:T(8,128)S(1)} %fusion.29), custom_call_target="Cholesky" | custom-call | tf_op jit(solution)/shard_map/jit(cholesky)/cholesky | solution.py:27
  310.1 9.8 %custom-call.9 = f32[1,128,128]{1,2,0:T(8,128)S(1)} custom-call(f32[1,128,128]{2,1,0:T(8,128)S(1)} %fusion.10), custom_call_target="InvertDiagBlocksLowerTriangular" | custom-call | tf_op jit(solution)/shard_map/jit(_cho_solve)/triangular_solve | solution.py:28
  320.5 1.0 fusion.35
  322.3 2.2 convolution_bitcast_fusion
  324.6 4.4 broadcast_select_fusion.1
  329.0 64.2 %all-reduce.17.cloned.1.call-done = (f32[2560,128]{1,0:T(8,128)}, f32[2560,128]{1,0:T(8,128)}) async-done(((f32[2560,128]{1,0:T(8,128)}, f32[2560,128]{1,0:T(8,128)}), (f32[2560,128]{1,0:T(8,128)}, f32[2560,128]{1,0:T(8,128)})) %all-reduce.17.cloned.1.call-update) | async-done | bytes 2621456 | tf_op jit(solution)/shard_map/psum | solution.py:9
  393.2 60.9 %convolution_bitcast_fusion.3 = f32[2560,128]{0,1:T(8,128)} fusion(f32[2560,5120]{1,0:T(8,128)} %param.10, f32[2560,128]{1,0:T(8,128)} %get-tuple-element.10, f32[2560,128]{1,0:T(8,128)} %get-tuple-element.11), kind=kOutput, calls=%fused_computation.7 | convolution fusion | flops 20133314560 | bytes 56360960 | tf_op jit(solution)/shard_map/dot_general | solution.py:13
  454.4 14.2 %fusion.37 = f32[128,1792]{1,0:T(8,128)} fusion(f32[128,2560]{1,0:T(8,128)S(1)} %copy-done, f32[2560,1792]{1,0:T(8,128)} %param.9), kind=kOutput, calls=%fused_computation.69 | convolution fusion | flops 7046430720 | bytes 20578304 | tf_op jit(solution)/shard_map/dot_general | solution.py:13
  468.6 2.9 convolution_bitcast_fusion.5
  471.5 42.5 %all-reduce.13.cloned.1.call-done = f32[2560,128]{0,1:T(8,128)} async-done(((f32[2560,128]{0,1:T(8,128)}), f32[2560,128]{0,1:T(8,128)}) %all-reduce.13.cloned.1.call-update) | async-done | bytes 1310736 | tf_op jit(solution)/shard_map/psum | solution.py:42
  514.0 4.2 fusion.36
  518.2 2.3 convolution_bitcast_fusion.1
  520.5 54.2 %all-reduce.15.cloned.1.call-done = (f32[128,128]{1,0:T(8,128)}, f32[128,128]{0,1:T(8,128)}, f32[128,1792]{1,0:T(8,128)}) async-done(((f32[128,128]{1,0:T(8,128)}, f32[128,128]{0,1:T(8,128)}, f32[128,1792]{1,0:T(8,128)}), (f32[128,128]{1,0:T(8,128)}, f32[128,128]{0,1:T(8,128)}, f32[128,1792]{1,0:T(8,128)})) %all-reduce.15.cloned.1.call-update) | async-done | bytes 1048592 | tf_op jit(solution)/shard_map/psum | solution.py:62
  574.7 1.2 convolution_add_fusion.1
  576.2 11.7 %cholesky.81 = f32[128,128]{1,0:T(8,128)S(1)} custom-call(f32[128,128]{1,0:T(8,128)S(1)} %fusion.17), custom_call_target="Cholesky" | custom-call | tf_op jit(solution)/shard_map/jit(cholesky)/cholesky | solution.py:27
  589.2 9.8 %custom-call.11 = f32[1,128,128]{1,2,0:T(8,128)S(1)} custom-call(f32[1,128,128]{2,1,0:T(8,128)S(1)} %fusion.12), custom_call_target="InvertDiagBlocksLowerTriangular" | custom-call | tf_op jit(solution)/shard_map/jit(_cho_solve)/triangular_solve | solution.py:28
  599.8 2.8 convolution_add_fusion
  602.6 17.4 %fusion.8 = f32[2560,1792]{1,0:T(8,128)} fusion(f32[2560,128]{0,1:T(8,128)S(1)} %convolution_add_fusion, f32[128,1792]{1,0:T(8,128)S(1)} %copy-done.5, f32[128,1792]{1,0:T(8,128)S(1)} %copy-done.6), kind=kOutput, calls=%fused_computation.21 | convolution fusion | flops 7046660096 | bytes 21495808 | tf_op jit(solution)/shard_map/dot_general | solution.py:13
  (55 shorter events, 10.5 us)
Async XLA Ops:
  6.5 37.8 %all-gather.2.cloned.1.call-start = ((), (), s32[]{:S(2)}) async-start(), calls=%async_computation | async-start | bytes 1638400 | tf_op jit(solution)/shard_map/all_gather | solution.py:46
  7.3 107.8 %all-reduce.21.cloned.1.call-start = ((), (), s32[]{:S(2)}) async-start(), calls=%async_computation.6 | async-start | bytes 5373952 | tf_op jit(solution)/shard_map/psum | solution.py:48
  46.1 1.9 copy-start.2
  46.1 2.3 copy-start
  50.2 185.8 %all-reduce.11.cloned.1.call-start = ((), (), s32[]{:S(2)}) async-start(), calls=%async_computation.1 | async-start | bytes 2621440 | tf_op jit(solution)/shard_map/psum | solution.py:42
  176.0 0.8 copy-start.4
  176.0 119.2 %all-reduce.19.cloned.1.call-start = ((), (), s32[]{:S(2)}) async-start(), calls=%async_computation.5 | async-start | bytes 262144 | tf_op jit(solution)/shard_map/psum | solution.py:51
  242.2 151.0 %all-reduce.17.cloned.1.call-start = ((), (), s32[]{:S(2)}) async-start(), calls=%async_computation.4 | async-start | bytes 5242880 | tf_op jit(solution)/shard_map/psum | solution.py:9
  322.3 2.3 copy-start.3
  329.0 185.0 %all-reduce.13.cloned.1.call-start = ((), (), s32[]{:S(2)}) async-start(), calls=%async_computation.2 | async-start | bytes 2621440 | tf_op jit(solution)/shard_map/psum | solution.py:42
  454.2 14.4 %copy-start.1 = (f32[2560,128]{1,0:T(8,128)S(1)}, f32[2560,128]{1,0:T(8,128)}, u32[]{:S(2)}) copy-start(f32[2560,128]{1,0:T(8,128)} %get-tuple-element.21) | copy-start | bytes 3932164
  454.2 120.6 %all-reduce.15.cloned.1.call-start = ((), (), s32[]{:S(2)}) async-start(), calls=%async_computation.3 | async-start | bytes 2097152 | tf_op jit(solution)/shard_map/psum | solution.py:62
  599.8 2.8 copy-start.5
  599.8 2.8 copy-start.6
Sparse Core Ops, SparseCore 0:
  8.9 35.3 all-gather.1
  50.3 64.7 all-reduce.20
  176.1 59.7 all-reduce.10
  242.4 52.7 all-reduce.18
  329.1 64.0 all-reduce.16
  454.3 59.6 all-reduce.12
  518.3 56.3 all-reduce.14
where the time goes:
time: 637 us; the launch traced here: 627 us
  waiting for transfers between devices  352 us (55%)
  matrix products  184 us (29%)
  other arithmetic  71.3 us (11%)
  between operations  14.2 us (2%)
    dot_general x12, matrix products, precise(): jnp.dot(left, right, precision=lax.Precision.HIGHEST, preferred_element_t...  173 us
    psum x2, waiting for transfers between devices, covariance_rows(): return lax.psum(precise(covariance, panel_rows), 'col')  89 us
    psum x1, waiting for transfers between devices, body(): lax.psum((precise(all_keys, weight), precise(all_keys, basis_panel)), 'row')  64.8 us
    psum x1, waiting for transfers between devices, spread(): return lax.psum(jnp.where(mine, value, jnp.zeros_like(value)), axis)  64.2 us
    psum x1, waiting for transfers between devices, body(): lax.psum((key_part, transposed_product(direction, cov_direction)), 'row')  54.2 us
    psum x1, waiting for transfers between devices, body(): lax.psum((transposed_product(basis_panel, image_one), transposed_product(...  42 us
    another operation x9, other arithmetic, definite_solve(): factor = jnp.linalg.cholesky(0.5 * (matrix + matrix.T))  37.3 us
    all_gather x1, waiting for transfers between devices, body(): all_keys = lax.all_gather(key_rows, 'col', axis=0, tiled=True)  37 us
  transfers between devices with their start and end apart: 7, of which 7 were waited for; matrix products, arithmetic and copies ran while one was open for 7% of the time, Pallas kernels for 0%

commit v1 on v0

v1 whole, which is shorter than its diff:
```python
import jax
import jax.numpy as jnp
from jax import lax
from jax.experimental import pallas as pl
from jax.experimental.pallas import tpu as pltpu
from jax.sharding import PartitionSpec as P

VMEM_LIMIT = 56 * 2**20
LANES = 128
ACROSS = (((1,), (1,)), ((), ()))
PLAIN = (((1,), (0,)), ((), ()))


def tile_of(extent, most):
    best = extent
    for tile in range(LANES, min(extent, most) + 1, LANES):
        if extent % tile == 0:
            best = tile
    return best


def split(value):
    high = value.astype(jnp.bfloat16)
    return high, (value - high.astype(jnp.float32)).astype(jnp.bfloat16)


def precise(left, right, dims=PLAIN):
    return lax.dot_general(
        left, right, dims, precision=lax.Precision.HIGHEST, preferred_element_type=jnp.float32
    )


def split_product(both, right, dims):
    count = both.shape[0] // 2
    high, low = split(right)
    wide = lax.dot_general(both, high, dims, preferred_element_type=jnp.float32)
    rest = lax.dot_general(both[:count], low, dims, preferred_element_type=jnp.float32)
    return wide[:count] + wide[count:] + rest


def settings(flops, moved):
    return dict(
        compiler_params=pltpu.CompilerParams(vmem_limit_bytes=VMEM_LIMIT),
        cost_estimate=pl.CostEstimate(flops=flops, bytes_accessed=moved, transcendentals=0),
    )


def floats(*shape):
    return jax.ShapeDtypeStruct(shape, jnp.float32)


def image_kernel(places_ref, keys_ref, block_ref, out_ref, both):
    count, depth = keys_ref.shape

    @pl.when(pl.program_id(0) == 0)
    def _():
        both[:count], both[count:] = split(keys_ref[...])

    step = tile_of(depth, 640)
    total = jnp.zeros(out_ref.shape[1:], jnp.float32)
    for start in range(0, depth, step):
        part = slice(start, start + step)
        total = total + split_product(both[:, part], block_ref[part, :], PLAIN)
    out_ref[0] = total


def image_pieces(keys, covariance, places, width):
    count, depth = keys.shape
    pieces = places.shape[0]
    if width % LANES:
        step = tile_of(covariance.shape[1], 640)
        full = image_pieces(
            keys, covariance, jnp.arange(covariance.shape[1] // step, dtype=jnp.int32), step
        )
        full = full.transpose(1, 0, 2).reshape(count, -1)
        return jnp.stack(
            [lax.dynamic_slice_in_dim(full, places[i] * width, width, 1) for i in range(pieces)]
        )
    return pl.pallas_call(
        image_kernel,
        out_shape=floats(pieces, count, width),
        grid_spec=pltpu.PrefetchScalarGridSpec(
            num_scalar_prefetch=1,
            grid=(pieces,),
            in_specs=[
                pl.BlockSpec((count, depth), lambda j, places: (0, 0)),
                pl.BlockSpec((depth, width), lambda j, places: (0, places[j])),
            ],
            out_specs=pl.BlockSpec((1, count, width), lambda j, places: (j, 0, 0)),
            scratch_shapes=[pltpu.VMEM((2 * count, depth), jnp.bfloat16)],
        ),
        **settings(6 * count * depth * width * pieces, 4 * depth * width * pieces),
    )(places, keys, covariance)


def apply_kernel(places_ref, order_ref, piece_ref, block_ref, *rest):
    *before, out_ref, both = rest
    count, width = piece_ref.shape[1:]
    shares, _, rows = out_ref.shape

    @pl.when(pl.program_id(0) == 0)
    def _():
        out_ref[...] = before[0][...] if before else jnp.zeros(out_ref.shape, jnp.float32)

    both[:count], both[count:] = split(piece_ref[0])
    for share in range(shares):
        start = pl.multiple_of(order_ref[share] * rows, 8)
        out_ref[share] += split_product(both[...], block_ref[pl.ds(start, rows), :], ACROSS)


def apply_pieces(pieces, covariance, places, order, before=None):
    number, count, width = pieces.shape
    depth, shares = covariance.shape[0], order.shape[0]
    rows = depth // shares
    if width % LANES:
        step = tile_of(covariance.shape[1], 640)
        full = jnp.zeros((count, covariance.shape[1]), jnp.float32)
        for i in range(number):
            full = lax.dynamic_update_slice_in_dim(full, pieces[i], places[i] * width, 1)
        full = full.reshape(count, -1, step).transpose(1, 0, 2)
        return apply_pieces(
            full, covariance, jnp.arange(full.shape[0], dtype=jnp.int32), order, before
        )
    whole = pl.BlockSpec((shares, count, rows), lambda j, places, order: (0, 0, 0))
    extra = [] if before is None else [before]
    return pl.pallas_call(
        apply_kernel,
        out_shape=floats(shares, count, rows),
        grid_spec=pltpu.PrefetchScalarGridSpec(
            num_scalar_prefetch=2,
            grid=(number,),
            in_specs=[
                pl.BlockSpec((1, count, width), lambda j, places, order: (j, 0, 0)),
                pl.BlockSpec((depth, width), lambda j, places, order: (0, places[j])),
                *[whole for _ in extra],
            ],
            out_specs=whole,
            scratch_shapes=[pltpu.VMEM((2 * count, width), jnp.bfloat16)],
        ),
        **settings(6 * count * depth * width * number, 4 * depth * width * number),
    )(places, order, pieces, covariance, *extra)


def fitted_kernel(places_ref, keys_ref, weight_ref, theirs_ref, mine_ref, sorted_keys, both):
    count = keys_ref.shape[0]
    pieces = places_ref.shape[0]
    rows, half = count // pieces, count // 2

    @pl.when(pl.program_id(0) == 0)
    def _():
        for i in range(pieces):
            start = pl.multiple_of(places_ref[i] * rows, 8)
            sorted_keys[i * rows : (i + 1) * rows, :] = keys_ref[pl.ds(start, rows), :]
        both[:count], both[count:] = split(sorted_keys[...])

    total = split_product(both[...], weight_ref[...], PLAIN)
    theirs_ref[...], mine_ref[...] = total[:half], total[half:]


def fitted_parts(keys, weight, places):
    count, depth = keys.shape
    width = weight.shape[1]
    tile = tile_of(width, 256)
    half = pl.BlockSpec((count // 2, tile), lambda j, places: (0, j))
    return pl.pallas_call(
        fitted_kernel,
        out_shape=[floats(count // 2, width)] * 2,
        grid_spec=pltpu.PrefetchScalarGridSpec(
            num_scalar_prefetch=1,
            grid=(width // tile,),
            in_specs=[
                pl.BlockSpec((count, depth), lambda j, places: (0, 0)),
                pl.BlockSpec((depth, tile), lambda j, places: (0, j)),
            ],
            out_specs=[half, half],
            scratch_shapes=[
                pltpu.VMEM((count, depth), jnp.float32),
                pltpu.VMEM((2 * count, depth), jnp.bfloat16),
            ],
        ),
        **settings(6 * count * depth * width, 4 * depth * width),
    )(places, keys, weight)


def moments_kernel(col_ref, keys_ref, piece_ref, share_ref, out_ref):
    width = share_ref.shape[1]
    out_ref[0] = precise(keys_ref[...], keys_ref[...], ACROSS)
    for i in range(keys_ref.shape[1] // width):

        @pl.when(col_ref[0] == i)
        def _():
            part = keys_ref[:, i * width : (i + 1) * width]
            out_ref[1] = precise(part, share_ref[...], ACROSS)

    out_ref[2] = precise(piece_ref[...], piece_ref[...], ACROSS)


def moments(keys, piece, share, col):
    count = keys.shape[0]
    return pl.pallas_call(
        moments_kernel,
        out_shape=floats(3, count, count),
        in_specs=[pl.BlockSpec(memory_space=pltpu.SMEM)]
        + [pl.BlockSpec(memory_space=pltpu.VMEM)] * 3,
        out_specs=pl.BlockSpec(memory_space=pltpu.VMEM),
        **settings(12 * count * count * keys.shape[1], 8 * keys.size),
    )(col.reshape(1), keys, piece, share)


def third_kernel(image_ref, *refs):
    *shares, out_ref = refs
    out_ref[...] = sum(
        precise(share[...], image_ref[i], ACROSS) for i, share in enumerate(shares)
    )


def third_moment(shares, image):
    count = image.shape[1]
    return pl.pallas_call(
        third_kernel,
        out_shape=floats(count, count),
        **settings(12 * count * image.size, 8 * image.size),
    )(image, *shares)


def eliminate(work, count):
    row = lax.broadcasted_iota(jnp.int32, (count, 1), 0)
    for k in range(count):
        pivot_row = work[k : k + 1, :]
        scaled = pivot_row * (1.0 / pivot_row[:, k : k + 1])
        factor = jnp.where(row == k, 0.0, work[:, k : k + 1])
        updated = work[...] - factor * scaled
        work[...] = jnp.where(row == k, scaled, updated)


def early_kernel(gram_ref, moments_ref, alpha_ref, basis_ref, right_ref, known_ref, work):
    count = gram_ref.shape[0]
    gram, first, second = gram_ref[...], moments_ref[0], moments_ref[1]
    first = 0.5 * (first + first.T)
    curvature = first + precise(gram, gram)
    three = precise(gram, jnp.concatenate([first, second, curvature], axis=1))
    gram_first, gram_second, gram_curvature = (
        three[:, i * count : (i + 1) * count] for i in range(3)
    )
    square = second + gram_first.T + gram_curvature
    work[:, :count] = 0.5 * (curvature + curvature.T)
    work[:, count : 2 * count] = square
    work[:, 2 * count :] = gram
    eliminate(work, count)
    moved, alpha = work[:, count : 2 * count], work[:, 2 * count :]
    two = precise(square, work[:, count:])
    alpha_ref[...] = alpha
    basis_ref[...] = gram - moved
    right_ref[...] = curvature - two[:, count:]
    known_ref[...] = (
        gram_second
        + gram_second.T
        + precise(gram_first, gram)
        + precise(curvature, curvature)
        - two[:, :count]
    )


def early_solve(gram, pair):
    count = gram.shape[0]
    return pl.pallas_call(
        early_kernel,
        out_shape=[floats(count, count)] * 4,
        scratch_shapes=[pltpu.VMEM((count, 3 * count), jnp.float32)],
        **settings(60 * count**3, 32 * count**2),
    )(gram, pair)


def late_kernel(
    places_ref, third_ref, known_ref, right_ref, alpha_ref, basis_ref, theirs_ref, mine_ref,
    targets_ref, high_ref, low_ref, work, residual,
):
    count = third_ref.shape[0]
    pieces = places_ref.shape[0]
    rows, half = count // pieces, count // 2
    for i in range(pieces):
        start = pl.multiple_of(places_ref[i] * rows, 8)
        source, at = (theirs_ref, i * rows) if i * rows < half else (mine_ref, i * rows - half)
        part = pl.ds(start, rows)
        residual[part, :] = targets_ref[part, :] - source[at : at + rows, :]
    matrix = third_ref[...] + known_ref[...]
    work[:, :count] = 0.5 * (matrix + matrix.T)
    work[:, count:] = right_ref[...]
    eliminate(work, count)
    lower = precise(work[:, count:], residual[...])
    upper = precise(alpha_ref[...], residual[...]) + precise(basis_ref[...], lower)
    high_ref[:count], low_ref[:count] = split(upper)
    high_ref[count:], low_ref[count:] = split(lower)


def late_solve(third, known, right, alpha, basis, theirs, mine, targets, places):
    count, width = targets.shape
    halves = jax.ShapeDtypeStruct((2 * count, width), jnp.bfloat16)
    return pl.pallas_call(
        late_kernel,
        out_shape=[halves, halves],
        in_specs=[pl.BlockSpec(memory_space=pltpu.SMEM)]
        + [pl.BlockSpec(memory_space=pltpu.VMEM)] * 8,
        scratch_shapes=[
            pltpu.VMEM((count, 2 * count), jnp.float32),
            pltpu.VMEM((count, width), jnp.float32),
        ],
        **settings(40 * count**3, 16 * count * width),
    )(places, third, known, right, alpha, basis, theirs, mine, targets)


def upright_kernel(order_ref, keys_ref, *refs):
    *shares, high_ref, low_ref = refs
    count = keys_ref.shape[0]
    high_ref[:, :count], low_ref[:, :count] = split(keys_ref[...].T)
    for i, share in enumerate(shares):
        rows = share.shape[1]
        part = pl.ds(pl.multiple_of(order_ref[i] * rows, 16), rows)
        high_ref[part, count:], low_ref[part, count:] = split(share[...].T)


def upright(keys, shares, order):
    count, depth = keys.shape
    tall = jax.ShapeDtypeStruct((depth, 2 * count), jnp.bfloat16)
    return pl.pallas_call(
        upright_kernel,
        out_shape=[tall, tall],
        in_specs=[pl.BlockSpec(memory_space=pltpu.SMEM)]
        + [pl.BlockSpec(memory_space=pltpu.VMEM)] * (1 + len(shares)),
        **settings(count * depth, 16 * count * depth),
    )(order, keys, *shares)


def increment_kernel(high_ref, low_ref, right_high_ref, right_low_ref, out_ref):
    out_ref[...] = (
        jnp.dot(high_ref[...], right_high_ref[...], preferred_element_type=jnp.float32)
        + jnp.dot(low_ref[...], right_high_ref[...], preferred_element_type=jnp.float32)
        + jnp.dot(high_ref[...], right_low_ref[...], preferred_element_type=jnp.float32)
    )


def increment_product(high, low, right_high, right_low):
    rows, depth = high.shape
    width = right_high.shape[1]
    tile = tile_of(rows, 256)
    left = pl.BlockSpec((tile, depth), lambda j: (j, 0))
    right = pl.BlockSpec((depth, width), lambda j: (0, 0))
    return pl.pallas_call(
        increment_kernel,
        out_shape=floats(rows, width),
        grid=(rows // tile,),
        in_specs=[left, left, right, right],
        out_specs=pl.BlockSpec((tile, width), lambda j: (j, 0)),
        **settings(6 * depth * rows * width, 4 * (depth * rows + depth * width + rows * width)),
    )(high, low, right_high, right_low)


def swap(value, mask):
    return lax.ppermute(value, "row", [(i, i ^ mask) for i in range(lax.axis_size("row"))])


def others(value):
    count = lax.axis_size("col")
    return [
        lax.ppermute(value, "col", [(i, (i + d) % count) for i in range(count)])
        for d in range(1, count)
    ]


def chip_masks():
    return range(2, lax.axis_size("row"), 2)


def sum_over_row(value):
    value = value + swap(value, 1)
    return sum((swap(value, mask) for mask in chip_masks()), value)


def sum_over_col(value):
    return sum(others(value), value)


def after(value, *earlier):
    return lax.optimization_barrier((value, *earlier))[0]


def to_rows(value, k):
    rows, cols = lax.axis_size("row"), lax.axis_size("col")
    blocks, chips = rows // cols, rows // 2
    pairs = []
    for row in range(rows):
        place = (row % 2) * chips + row // 2
        for col in range(cols):
            target = (blocks * col + place // cols) * cols + (place % cols - k) % cols
            pairs.append((row * cols + col, target))
    return lax.ppermute(value, ("row", "col"), pairs)


def body(key_rows, targets, weight, covariance):
    rows, cols = lax.axis_size("row"), lax.axis_size("col")
    row, col = lax.axis_index("row"), lax.axis_index("col")
    chips, core, chip = rows // 2, row % 2, row // 2
    count = key_rows.shape[0] * cols
    width = covariance.shape[1] // rows
    near = jnp.bitwise_xor(jnp.arange(chips, dtype=jnp.int32), chip)
    mine, theirs = core * chips + near, (1 - core) * chips + near
    order = (col + jnp.arange(cols, dtype=jnp.int32)) % cols

    keys = jnp.zeros((cols, *key_rows.shape), key_rows.dtype)
    for d, block in enumerate([key_rows, *others(key_rows)]):
        keys = lax.dynamic_update_index_in_dim(keys, block, (col - d) % cols, 0)
    keys = keys.reshape(count, -1)

    far_part = image_pieces(keys, covariance, theirs, width)
    near_part = image_pieces(after(keys, far_part), covariance, mine, width)
    part = near_part + swap(far_part, 1)
    piece = sum((swap(part[mask // 2], mask) for mask in chip_masks()), part[0])

    fitted_theirs, fitted_mine = fitted_parts(
        after(keys, near_part), weight, jnp.concatenate([theirs, mine])
    )

    near_pieces = jnp.stack([piece, *[swap(piece, mask) for mask in chip_masks()]])
    shares = [to_rows(piece, k) for k in range(cols)]
    far_pieces = swap(near_pieces, 1)

    fitted = fitted_mine + swap(fitted_theirs, 1)
    height = count // rows
    fitted = fitted.reshape(chips, height, -1)
    fitted = sum((swap(fitted[mask // 2], mask) for mask in chip_masks()), fitted[0])
    fitted_mine = jnp.concatenate([fitted, *[swap(fitted, mask) for mask in chip_masks()]], axis=0)
    fitted_theirs = swap(fitted_mine, 1)

    sums = sum_over_row(moments(keys, piece, shares[0], col))
    gram, pair = sums[0], sum_over_col(sums[1:])
    alpha, basis, right, known = early_solve(gram, pair)

    applied = apply_pieces(near_pieces, covariance, mine, order)
    applied = apply_pieces(far_pieces, covariance, theirs, order, applied)
    third = sum_over_col(sum_over_row(third_moment(shares, applied)))
    tall_high, tall_low = upright(keys, shares, order)

    high, low = late_solve(
        third, known, right, alpha, basis, fitted_theirs, fitted_mine, targets,
        jnp.concatenate([theirs, mine]),
    )
    return increment_product(tall_high, tall_low, high, low)


def solution(mesh):
    placed = (P("col", "row"), P(None, "col"), P("row", "col"), P("row", "col"))
    return jax.shard_map(
        body, mesh=mesh, in_specs=placed, out_specs=P("row", "col"), check_vma=False
    )
```

time: 637 us -> 265 us (0.42); the launches traced: 627 us -> 264 us
  waiting for transfers between devices: 352 us -> 68.1 us
  matrix products: 184 us -> 0 us
  Pallas kernels: 0 us -> 127 us
  other arithmetic: 71.3 us -> 4.44 us
  starting transfers between devices: 1.08 us -> 57.4 us
  between operations: 14.2 us -> 0.38 us
    psum x6 -> x0, waiting for transfers between devices: 314 us -> none  [the longest x2 89 us: covariance_rows(): return lax.psum(precise(covariance, panel_rows), 'col')]
    dot_general x17 -> x0, matrix products: 183 us -> none  [the longest x12 173 us: precise(): jnp.dot(left, right, precision=lax.Precision.HIGHEST, preferred_element_t...]
    pallas_call x0 -> x11, Pallas kernels: none -> 127 us  [the longest x2 30.6 us: apply_pieces(): pl.pallas_call(apply_kernel, out_shape=floats(shares, count, rows), grid_...]
    another operation x15 -> x1, other arithmetic: 68.7 us -> 0.09 us  [body(): jnp.stack([piece, *[swap(piece, mask) for mask in chip_masks()]])]
    ppermute x0 -> x37, waiting for transfers between devices: none -> 68.1 us  [the longest x24 35.3 us: swap(): lax.ppermute(value, 'row', [(i, i ^ mask) for i in range(lax.axis_size('r...]
    ppermute x0 -> x37, starting transfers between devices: none -> 57.4 us  [the longest x24 32.4 us: swap(): lax.ppermute(value, 'row', [(i, i ^ mask) for i in range(lax.axis_size('r...]
    all_gather x1 -> x0, waiting for transfers between devices: 37 us -> none  [body(): all_keys = lax.all_gather(key_rows, 'col', axis=0, tiled=True)]
  transfers between devices with their start and end apart: 7 -> 37, of which waited for: 7 -> 18; matrix products, arithmetic and copies ran while one was open for 7% -> 2% of each run, Pallas kernels for 0% -> 31%
where the time goes in v1:
time: 265 us; the launch traced here: 264 us
  Pallas kernels  127 us (48%)
  waiting for transfers between devices  68.1 us (26%)
  starting transfers between devices  57.4 us (22%)
  local copies, waits for them, and re-layouts  6.06 us (2%)
  other arithmetic  4.44 us (2%)
    ppermute x24, waiting for transfers between devices, swap(): lax.ppermute(value, 'row', [(i, i ^ mask) for i in range(lax.axis_size('r...  35.3 us
    ppermute x9, waiting for transfers between devices, others(): lax.ppermute(value, 'col', [(i, (i + d) % count) for i in range(count)])  32.8 us
    ppermute x24, starting transfers between devices, swap(): lax.ppermute(value, 'row', [(i, i ^ mask) for i in range(lax.axis_size('r...  32.4 us
    pallas_call x2, Pallas kernels, apply_pieces(): pl.pallas_call(apply_kernel, out_shape=floats(shares, count, rows), grid_...  30.6 us
    pallas_call x2, Pallas kernels, image_pieces(): pl.pallas_call(image_kernel, out_shape=floats(pieces, count, width), grid...  28.3 us
    pallas_call x1, Pallas kernels, late_solve(): pl.pallas_call(late_kernel, out_shape=[halves, halves], in_specs=[pl.Bloc...  16.7 us
    pallas_call x1, Pallas kernels, increment_product(): pl.pallas_call(increment_kernel, out_shape=floats(rows, width), grid=(row...  14 us
    pallas_call x1, Pallas kernels, early_solve(): pl.pallas_call(early_kernel, out_shape=[floats(count, count)] * 4, scratc...  13.6 us
  transfers between devices with their start and end apart: 37, of which 18 were waited for; matrix products, arithmetic and copies ran while one was open for 2% of the time, Pallas kernels for 31%

profile of v1, /device:TPU:0, one launch (start us, length us, event | category | flops | bytes accessed | tf_op | source)
XLA Modules:
  0.0 263.8 jit_solution(5692570495200157598)
XLA Ops:
  0.0 3.0 %collective-permute-start = (f32[32,2560]{1,0:T(8,128)}, f32[32,2560]{1,0:T(8,128)S(1)}, u32[]{:S(2)}, u32[]{:S(2)}) collective-permute-start(f32[32,2560]{1,0:T(8,128)} %param.4), channel_id=1, source_target_pairs={{0,1},{1,2},{2,3},{3,0},{4,5},{5,6},{6,7},{7,4},{8,9},{9,10},{10,1... | collective-permute-start | bytes 983048 | tf_op jit(solution)/shard_map/ppermute | solution.py:365
  3.0 2.1 collective-permute-start.2
  6.8 7.1 %collective-permute-done = f32[32,2560]{1,0:T(8,128)S(1)} collective-permute-done((f32[32,2560]{1,0:T(8,128)}, f32[32,2560]{1,0:T(8,128)S(1)}, u32[]{:S(2)}, u32[]{:S(2)}) %collective-permute-start) | collective-permute-done | bytes 327712 | tf_op jit(solution)/shard_map/ppermute | solution.py:365
  13.9 20.2 %collective-permute-done.1 = f32[32,2560]{1,0:T(8,128)S(1)} collective-permute-done((f32[32,2560]{1,0:T(8,128)}, f32[32,2560]{1,0:T(8,128)S(1)}, u32[]{:S(2)}, u32[]{:S(2)}) %collective-permute-start.1) | collective-permute-done | bytes 327712 | tf_op jit(solution)/shard_map/ppermute | solution.py:365
  35.2 14.3 %shard_map.46 = f32[4,128,640]{2,1,0:T(8,128)} custom-call(s32[4]{0:T(128)} %fusion.6.places_ref, f32[128,2560]{1,0:T(8,128)} %bitcast.30, f32[2560,5120]{1,0:T(8,128)} %block_ref.7), custom_call_target="tpu_custom_call" | custom-call | flops 5033164800 | bytes 26214400 | tf_op jit(solution)/shard_map/pallas_call | solution.py:79
  50.2 14.0 %shard_map.47 = f32[4,128,640]{2,1,0:T(8,128)} custom-call(s32[4]{0:T(128)} %copy-done.14, f32[128,2560]{1,0:T(8,128)} %bitcast.31, f32[2560,5120]{1,0:T(8,128)} %block_ref.7), custom_call_target="tpu_custom_call" | custom-call | flops 5033164800 | bytes 26214400 | tf_op jit(solution)/shard_map/pallas_call | solution.py:79
  64.3 12.1 %shard_map.54 = (f32[64,1792]{1,0:T(8,128)}, f32[64,1792]{1,0:T(8,128)}) custom-call(s32[8]{0:T(128)} %pad_add_fusion.places_ref, f32[128,2560]{1,0:T(8,128)} %bitcast.32, f32[2560,1792]{1,0:T(8,128)} %weight_ref.1), custom_call_target="tpu_custom_call" | custom-call | flops 3523215360 | bytes 18350080 | tf_op jit(solution)/shard_map/pallas_call | solution.py:165
  78.3 1.6 collective-permute-start.6
  80.7 7.0 %collective-permute-done.4 = f32[128,640]{1,0:T(8,128)S(1)} collective-permute-done((f32[128,640]{1,0:T(8,128)S(1)}, f32[128,640]{1,0:T(8,128)S(1)}, u32[]{:S(2)}, u32[]{:S(2)}) %collective-permute-start.4) | collective-permute-done | bytes 327712 | tf_op jit(solution)/shard_map/ppermute | solution.py:359
  87.7 6.9 %collective-permute-done.6 = f32[128,640]{1,0:T(8,128)S(1)} collective-permute-done((f32[128,640]{1,0:T(8,128)S(1)}, f32[128,640]{1,0:T(8,128)S(1)}, u32[]{:S(2)}, u32[]{:S(2)}) %collective-permute-start.6) | collective-permute-done | bytes 327712 | tf_op jit(solution)/shard_map/ppermute | solution.py:359
  97.5 1.7 collective-permute-start.12
  99.7 1.6 collective-permute-start.30
  102.0 5.8 %collective-permute-done.13 = f32[128,640]{1,0:T(8,128)S(1)} collective-permute-done((f32[128,640]{1,0:T(8,128)S(1)}, f32[128,640]{1,0:T(8,128)S(1)}, u32[]{:S(2)}, u32[]{:S(2)}) %collective-permute-start.13) | collective-permute-done | bytes 327712 | tf_op jit(solution)/shard_map/ppermute | solution.py:359
  108.5 3.9 %collective-permute-done.12 = f32[128,640]{1,0:T(8,128)S(1)} collective-permute-done((f32[128,640]{1,0:T(8,128)S(1)}, f32[128,640]{1,0:T(8,128)S(1)}, u32[]{:S(2)}, u32[]{:S(2)}) %collective-permute-start.12) | collective-permute-done | bytes 327712 | tf_op jit(solution)/shard_map/ppermute | solution.py:359
  114.5 1.9 collective-permute-done.32
  117.8 1.7 collective-permute-start.34
  124.3 10.9 %collective-permute-start.10 = (f32[128,640]{1,0:T(8,128)S(1)}, f32[128,640]{1,0:T(8,128)S(1)}, u32[]{:S(2)}, u32[]{:S(2)}) collective-permute-start(f32[128,640]{1,0:T(8,128)S(1)} %fusion.2.piece_ref), channel_id=1, source_target_pairs={{0,1},{1,9},{2,17},{3,25},{4,5},{5,13},{6,21},{7,29},{8,2},{9,10},... | collective-permute-start | bytes 983048 | tf_op jit(solution)/shard_map/ppermute | solution.py:396
  136.0 4.6 %shard_map.52 = f32[3,128,128]{2,1,0:T(8,128)} custom-call(s32[1]{0:T(128)} %bitcast.13.col_ref, f32[128,2560]{1,0:T(8,128)} %bitcast.33, f32[128,640]{1,0:T(8,128)} %copy-done.3, f32[128,640]{1,0:T(8,128)} %copy-done.4), custom_call_target="tpu_custom_call" | custom-call | flops 503316480 | bytes 2621440 | tf_op jit(solution)/shard_map/pallas_call | solution.py:200
  140.7 15.1 %shard_map.49.rest_0_ = f32[4,128,640]{2,1,0:T(8,128)} custom-call(s32[4]{0:T(128)} %copy-done.14, s32[4]{0:T(128)} %and_select_fusion.order_ref, f32[4,128,640]{2,1,0:T(8,128)} %copy-done.1, f32[2560,5120]{1,0:T(8,128)} %block_ref.7), custom_call_target="tpu_custom_call" | custom-call | flops 5033164800 | bytes 26214400 | tf_op jit(solution)/shard_map/pallas_call | solution.py:126
  157.9 3.9 %shard_map.48 = (bf16[2560,256]{1,0:T(8,128)(2,1)}, bf16[2560,256]{1,0:T(8,128)(2,1)}) custom-call(s32[4]{0:T(128)} %and_select_fusion.order_ref, f32[128,2560]{1,0:T(8,128)} %bitcast.34, f32[128,640]{1,0:T(8,128)} %copy-done.4, f32[128,640]{1,0:T(8,128)} %copy-done.8, f32[128,640]{1,0:T(8,128)} %copy-done.7, f32[128,640]{1,0:T(8,128)} %copy-done.6), custom_call_target="tpu_custom_call" | custom-call | flops 327680 | bytes 5242880 | tf_op jit(solution)/shard_map/pallas_call | solution.py:325
  161.8 2.5 collective-permute-start.25
  164.3 9.9 %collective-permute-start.24 = (f32[3,128,128]{2,1,0:T(8,128)S(1)}, f32[3,128,128]{2,1,0:T(8,128)S(1)}, u32[]{:S(2)}, u32[]{:S(2)}) collective-permute-start(f32[3,128,128]{2,1,0:T(8,128)S(1)} %add.150), channel_id=1, source_target_pairs={{0,16},{4,20},{8,24},{12,28},{16,0},{20,4},{24,8},{28,12},{1,17},{... | collective-permute-start | bytes 589832 | tf_op jit(solution)/shard_map/ppermute | solution.py:359
  176.7 15.5 %shard_map.50.image_ref = f32[4,128,640]{2,1,0:T(8,128)} custom-call(s32[4]{0:T(128)} %fusion.6.places_ref, s32[4]{0:T(128)} %and_select_fusion.order_ref, f32[4,128,640]{2,1,0:T(8,128)} %copy-done.9, f32[2560,5120]{1,0:T(8,128)} %block_ref.7, f32[4,128,640]{2,1,0:T(8,128)} %shard_map.49.rest_0_), custom_call_target="tpu_custom_call" | custom-call | flops 5033164800 | bytes 26214400 | tf_op jit(solution)/shard_map/pallas_call | solution.py:126
  192.2 3.8 %shard_map.51 = f32[128,128]{1,0:T(8,128)} custom-call(f32[4,128,640]{2,1,0:T(8,128)} %shard_map.50.image_ref, f32[128,640]{1,0:T(8,128)} %copy-done.4, f32[128,640]{1,0:T(8,128)} %copy-done.8, f32[128,640]{1,0:T(8,128)} %copy-done.7, f32[128,640]{1,0:T(8,128)} %copy-done.6), custom_call_target="tpu_custom_call" | custom-call | flops 503316480 | bytes 2621440 | tf_op jit(solution)/shard_map/pallas_call | solution.py:219
  198.3 1.5 collective-permute-start.18
  205.6 3.1 %collective-permute-start.21 = (f32[128,128]{1,0:T(8,128)S(1)}, f32[128,128]{1,0:T(8,128)S(1)}, u32[]{:S(2)}, u32[]{:S(2)}) collective-permute-start(f32[128,128]{1,0:T(8,128)S(1)} %add_add_fusion.3), channel_id=1, source_target_pairs={{0,3},{1,0},{2,1},{3,2},{4,7},{5,4},{6,5},{7,6},{8,11},{9,8},{10,9... | collective-permute-start | bytes 196616 | tf_op jit(solution)/shard_map/ppermute | solution.py:365
  208.7 1.9 collective-permute-done.27
  210.7 3.6 %collective-permute-done.28 = f32[2,128,128]{2,1,0:T(8,128)S(1)} collective-permute-done((f32[2,128,128]{2,1,0:T(8,128)S(1)}, f32[2,128,128]{2,1,0:T(8,128)S(1)}, u32[]{:S(2)}, u32[]{:S(2)}) %collective-permute-start.28) | collective-permute-done | bytes 131104 | tf_op jit(solution)/shard_map/ppermute | solution.py:365
  214.2 3.3 %collective-permute-start.19 = (f32[128,128]{1,0:T(8,128)S(1)}, f32[128,128]{1,0:T(8,128)S(1)}, u32[]{:S(2)}, u32[]{:S(2)}) collective-permute-start(f32[128,128]{1,0:T(8,128)S(1)} %add_add_fusion.3), channel_id=1, source_target_pairs={{0,1},{1,2},{2,3},{3,0},{4,5},{5,6},{6,7},{7,4},{8,9},{9,10},{10,1... | collective-permute-start | bytes 196616 | tf_op jit(solution)/shard_map/ppermute | solution.py:365
  218.2 13.6 %shard_map.53 = (f32[128,128]{1,0:T(8,128)}, f32[128,128]{1,0:T(8,128)}, f32[128,128]{1,0:T(8,128)}, f32[128,128]{1,0:T(8,128)}) custom-call(f32[128,128]{1,0:T(8,128)} %slice_bitcast_fusion.4.gram_ref, f32[2,128,128]{2,1,0:T(8,128)} %add_add_fusion.1.moments_ref), custom_call_target="tpu_custom_call" | custom-call | flops 125829120 | bytes 524288 | tf_op jit(solution)/shard_map/pallas_call | solution.py:266
  233.2 16.7 %shard_map.55 = (bf16[256,1792]{1,0:T(8,128)(2,1)}, bf16[256,1792]{1,0:T(8,128)(2,1)}) custom-call(s32[8]{0:T(128)} %pad_add_fusion.places_ref, f32[128,128]{1,0:T(8,128)} %add_add_fusion.2.third_ref, f32[128,128]{1,0:T(8,128)} %get-tuple-element.20.known_ref, f32[128,128]{1,0:T(8,128)} %get-tuple-element.21.right_ref, ...), custom_call_target="tpu_custom_call" | custom-call | flops 83886080 | bytes 3670016 | tf_op jit(solution)/shard_map/pallas_call | solution.py:299
  249.8 14.0 %shard_map.56 = f32[2560,1792]{1,0:T(8,128)} custom-call(bf16[2560,256]{1,0:T(8,128)(2,1)} %get-tuple-element.18.high_ref, bf16[2560,256]{1,0:T(8,128)(2,1)} %get-tuple-element.19.low_ref, bf16[256,1792]{1,0:T(8,128)(2,1)} %get-tuple-element.27.right_high_ref, bf16[256,1792]{1,0:T(8,128)(2,1)} %get-tuple-element.28.right_low_ref), custom_call_target="tpu_custom_call" | custom-call | flops 7046430720 | bytes 22806528 | tf_op jit(solution)/shard_map/pallas_call | solution.py:348
  (110 shorter events, 34.9 us)
Async XLA Ops:
  0.0 13.9 %collective-permute-start = (f32[32,2560]{1,0:T(8,128)}, f32[32,2560]{1,0:T(8,128)S(1)}, u32[]{:S(2)}, u32[]{:S(2)}) collective-permute-start(f32[32,2560]{1,0:T(8,128)} %param.4), channel_id=1, source_target_pairs={{0,1},{1,2},{2,3},{3,0},{4,5},{5,6},{6,7},{7,4},{8,9},{9,10},{10,1... | collective-permute-start | bytes 983048 | tf_op jit(solution)/shard_map/ppermute | solution.py:365
  3.0 31.1 %collective-permute-start.2 = (f32[32,2560]{1,0:T(8,128)}, f32[32,2560]{1,0:T(8,128)S(1)}, u32[]{:S(2)}, u32[]{:S(2)}) collective-permute-start(f32[32,2560]{1,0:T(8,128)} %param.4), channel_id=1, source_target_pairs={{0,3},{1,0},{2,1},{3,2},{4,7},{5,4},{6,5},{7,6},{8,11},{9,8},{10,9... | collective-permute-start | bytes 983048 | tf_op jit(solution)/shard_map/ppermute | solution.py:365
  5.1 29.0 %collective-permute-start.1 = (f32[32,2560]{1,0:T(8,128)}, f32[32,2560]{1,0:T(8,128)S(1)}, u32[]{:S(2)}, u32[]{:S(2)}) collective-permute-start(f32[32,2560]{1,0:T(8,128)} %param.4), channel_id=1, source_target_pairs={{0,2},{1,3},{2,0},{3,1},{4,6},{5,7},{6,4},{7,5},{8,10},{9,11},{10,... | collective-permute-start | bytes 983048 | tf_op jit(solution)/shard_map/ppermute | solution.py:365
  49.5 27.4 %collective-permute-start.3 = (f32[4,128,640]{2,1,0:T(8,128)}, f32[4,128,640]{2,1,0:T(8,128)S(1)}, u32[]{:S(2)}, u32[]{:S(2)}) collective-permute-start(f32[4,128,640]{2,1,0:T(8,128)} %shard_map.46), channel_id=1, source_target_pairs={{0,4},{4,0},{8,12},{12,8},{16,20},{20,16},{24,28},{28,24},{1,5},{5... | collective-permute-start | bytes 3932168 | tf_op jit(solution)/shard_map/ppermute | solution.py:359
  77.1 10.6 %collective-permute-start.4 = (f32[128,640]{1,0:T(8,128)S(1)}, f32[128,640]{1,0:T(8,128)S(1)}, u32[]{:S(2)}, u32[]{:S(2)}) collective-permute-start(f32[128,640]{1,0:T(8,128)S(1)} %get-tuple-element.29), channel_id=1, source_target_pairs={{0,8},{4,12},{8,0},{12,4},{16,24},{20,28},{24,16},{28,20},{1,9},{5... | collective-permute-start | bytes 983048 | tf_op jit(solution)/shard_map/ppermute | solution.py:359
  78.3 16.3 %collective-permute-start.6 = (f32[128,640]{1,0:T(8,128)S(1)}, f32[128,640]{1,0:T(8,128)S(1)}, u32[]{:S(2)}, u32[]{:S(2)}) collective-permute-start(f32[128,640]{1,0:T(8,128)S(1)} %get-tuple-element.30), channel_id=1, source_target_pairs={{0,24},{4,28},{8,16},{12,20},{16,8},{20,12},{24,0},{28,4},{1,25},{... | collective-permute-start | bytes 983048 | tf_op jit(solution)/shard_map/ppermute | solution.py:359
  79.9 16.1 %collective-permute-start.5 = (f32[128,640]{1,0:T(8,128)S(1)}, f32[128,640]{1,0:T(8,128)S(1)}, u32[]{:S(2)}, u32[]{:S(2)}) collective-permute-start(f32[128,640]{1,0:T(8,128)S(1)} %get-tuple-element.31), channel_id=1, source_target_pairs={{0,16},{4,20},{8,24},{12,28},{16,0},{20,4},{24,8},{28,12},{1,17},{... | collective-permute-start | bytes 983048 | tf_op jit(solution)/shard_map/ppermute | solution.py:359
  96.1 11.6 %collective-permute-start.13 = (f32[128,640]{1,0:T(8,128)S(1)}, f32[128,640]{1,0:T(8,128)S(1)}, u32[]{:S(2)}, u32[]{:S(2)}) collective-permute-start(f32[128,640]{1,0:T(8,128)S(1)} %fusion.2.piece_ref), channel_id=1, source_target_pairs={{0,24},{4,28},{8,16},{12,20},{16,8},{20,12},{24,0},{28,4},{1,25},{... | collective-permute-start | bytes 983048 | tf_op jit(solution)/shard_map/ppermute | solution.py:359
  97.5 14.9 %collective-permute-start.12 = (f32[128,640]{1,0:T(8,128)S(1)}, f32[128,640]{1,0:T(8,128)S(1)}, u32[]{:S(2)}, u32[]{:S(2)}) collective-permute-start(f32[128,640]{1,0:T(8,128)S(1)} %fusion.2.piece_ref), channel_id=1, source_target_pairs={{0,16},{4,20},{8,24},{12,28},{16,0},{20,4},{24,8},{28,12},{1,17},{... | collective-permute-start | bytes 983048 | tf_op jit(solution)/shard_map/ppermute | solution.py:359
  99.2 14.1 %collective-permute-start.11 = (f32[128,640]{1,0:T(8,128)S(1)}, f32[128,640]{1,0:T(8,128)S(1)}, u32[]{:S(2)}, u32[]{:S(2)}) collective-permute-start(f32[128,640]{1,0:T(8,128)S(1)} %fusion.2.piece_ref), channel_id=1, source_target_pairs={{0,8},{4,12},{8,0},{12,4},{16,24},{20,28},{24,16},{28,20},{1,9},{5... | collective-permute-start | bytes 983048 | tf_op jit(solution)/shard_map/ppermute | solution.py:359
  99.7 14.8 %collective-permute-start.30 = (f32[16,1792]{1,0:T(8,128)S(1)}, f32[16,1792]{1,0:T(8,128)S(1)}, u32[]{:S(2)}, u32[]{:S(2)}) collective-permute-start(f32[16,1792]{1,0:T(8,128)S(1)} %get-tuple-element.32), channel_id=1, source_target_pairs={{0,8},{4,12},{8,0},{12,4},{16,24},{20,28},{24,16},{28,20},{1,9},{5... | collective-permute-start | bytes 344072 | tf_op jit(solution)/shard_map/ppermute | solution.py:359
  101.3 15.1 %collective-permute-start.32 = (f32[16,1792]{1,0:T(8,128)S(1)}, f32[16,1792]{1,0:T(8,128)S(1)}, u32[]{:S(2)}, u32[]{:S(2)}) collective-permute-start(f32[16,1792]{1,0:T(8,128)S(1)} %get-tuple-element.33), channel_id=1, source_target_pairs={{0,24},{4,28},{8,16},{12,20},{16,8},{20,12},{24,0},{28,4},{1,25},{... | collective-permute-start | bytes 344072 | tf_op jit(solution)/shard_map/ppermute | solution.py:359
  107.7 8.7 %collective-permute-start.31 = (f32[16,1792]{1,0:T(8,128)S(1)}, f32[16,1792]{1,0:T(8,128)S(1)}, u32[]{:S(2)}, u32[]{:S(2)}) collective-permute-start(f32[16,1792]{1,0:T(8,128)S(1)} %get-tuple-element.34), channel_id=1, source_target_pairs={{0,16},{4,20},{8,24},{12,28},{16,0},{20,4},{24,8},{28,12},{1,17},{... | collective-permute-start | bytes 344072 | tf_op jit(solution)/shard_map/ppermute | solution.py:359
  113.4 62.3 %collective-permute-start.14 = (f32[4,128,640]{2,1,0:T(8,128)S(1)}, f32[4,128,640]{2,1,0:T(8,128)S(1)}, u32[]{:S(2)}, u32[]{:S(2)}) collective-permute-start(f32[4,128,640]{2,1,0:T(8,128)S(1)} %pad_maximum_fusion.piece_ref), channel_id=1, source_target_pairs={{0,4},{4,0},{8,12},{12,8},{16,20},{20,16},{24,28},{28,24},{1,5},{5... | collective-permute-start | bytes 3932168 | tf_op jit(solution)/shard_map/ppermute | solution.py:359
  116.5 6.1 %collective-permute-start.35 = (f32[16,1792]{1,0:T(8,128)S(1)}, f32[16,1792]{1,0:T(8,128)S(1)}, u32[]{:S(2)}, u32[]{:S(2)}) collective-permute-start(f32[16,1792]{1,0:T(8,128)S(1)} %fusion.4), channel_id=1, source_target_pairs={{0,24},{4,28},{8,16},{12,20},{16,8},{20,12},{24,0},{28,4},{1,25},{... | collective-permute-start | bytes 344072 | tf_op jit(solution)/shard_map/ppermute | solution.py:359
  117.8 5.8 %collective-permute-start.34 = (f32[16,1792]{1,0:T(8,128)S(1)}, f32[16,1792]{1,0:T(8,128)S(1)}, u32[]{:S(2)}, u32[]{:S(2)}) collective-permute-start(f32[16,1792]{1,0:T(8,128)S(1)} %fusion.4), channel_id=1, source_target_pairs={{0,16},{4,20},{8,24},{12,28},{16,0},{20,4},{24,8},{28,12},{1,17},{... | collective-permute-start | bytes 344072 | tf_op jit(solution)/shard_map/ppermute | solution.py:359
  120.0 15.2 %collective-permute-start.7 = (f32[128,640]{1,0:T(8,128)S(1)}, f32[128,640]{1,0:T(8,128)S(1)}, u32[]{:S(2)}, u32[]{:S(2)}) collective-permute-start(f32[128,640]{1,0:T(8,128)S(1)} %fusion.2.piece_ref), channel_id=1, source_target_pairs={{0,0},{1,8},{2,16},{3,24},{4,4},{5,12},{6,20},{7,28},{8,1},{9,9},{... | collective-permute-start | bytes 983048 | tf_op jit(solution)/shard_map/ppermute | solution.py:396
  124.3 31.4 %collective-permute-start.10 = (f32[128,640]{1,0:T(8,128)S(1)}, f32[128,640]{1,0:T(8,128)S(1)}, u32[]{:S(2)}, u32[]{:S(2)}) collective-permute-start(f32[128,640]{1,0:T(8,128)S(1)} %fusion.2.piece_ref), channel_id=1, source_target_pairs={{0,1},{1,9},{2,17},{3,25},{4,5},{5,13},{6,21},{7,29},{8,2},{9,10},... | collective-permute-start | bytes 983048 | tf_op jit(solution)/shard_map/ppermute | solution.py:396
  135.2 21.2 %collective-permute-start.9 = (f32[128,640]{1,0:T(8,128)S(1)}, f32[128,640]{1,0:T(8,128)S(1)}, u32[]{:S(2)}, u32[]{:S(2)}) collective-permute-start(f32[128,640]{1,0:T(8,128)S(1)} %fusion.2.piece_ref), channel_id=1, source_target_pairs={{0,2},{1,10},{2,18},{3,26},{4,6},{5,14},{6,22},{7,30},{8,3},{9,11}... | collective-permute-start | bytes 983048 | tf_op jit(solution)/shard_map/ppermute | solution.py:396
  135.2 21.2 %collective-permute-start.8 = (f32[128,640]{1,0:T(8,128)S(1)}, f32[128,640]{1,0:T(8,128)S(1)}, u32[]{:S(2)}, u32[]{:S(2)}) collective-permute-start(f32[128,640]{1,0:T(8,128)S(1)} %fusion.2.piece_ref), channel_id=1, source_target_pairs={{0,3},{1,11},{2,19},{3,27},{4,7},{5,15},{6,23},{7,31},{8,0},{9,8},... | collective-permute-start | bytes 983048 | tf_op jit(solution)/shard_map/ppermute | solution.py:396
  140.6 21.2 %collective-permute-start.22 = (f32[3,128,128]{2,1,0:T(8,128)}, f32[3,128,128]{2,1,0:T(8,128)S(1)}, u32[]{:S(2)}, u32[]{:S(2)}) collective-permute-start(f32[3,128,128]{2,1,0:T(8,128)} %shard_map.52), channel_id=1, source_target_pairs={{0,4},{4,0},{8,12},{12,8},{16,20},{20,16},{24,28},{28,24},{1,5},{5... | collective-permute-start | bytes 589832 | tf_op jit(solution)/shard_map/ppermute | solution.py:359
  155.7 76.7 %collective-permute-start.36 = (f32[64,1792]{1,0:T(8,128)S(1)}, f32[64,1792]{1,0:T(8,128)S(1)}, u32[]{:S(2)}, u32[]{:S(2)}) collective-permute-start(f32[64,1792]{1,0:T(8,128)S(1)} %pad_maximum_fusion.1.mine_ref), channel_id=1, source_target_pairs={{0,4},{4,0},{8,12},{12,8},{16,20},{20,16},{24,28},{28,24},{1,5},{5... | collective-permute-start | bytes 1376264 | tf_op jit(solution)/shard_map/ppermute | solution.py:359
  161.8 34.1 %collective-permute-start.25 = (f32[3,128,128]{2,1,0:T(8,128)S(1)}, f32[3,128,128]{2,1,0:T(8,128)S(1)}, u32[]{:S(2)}, u32[]{:S(2)}) collective-permute-start(f32[3,128,128]{2,1,0:T(8,128)S(1)} %add.150), channel_id=1, source_target_pairs={{0,24},{4,28},{8,16},{12,20},{16,8},{20,12},{24,0},{28,4},{1,25},{... | collective-permute-start | bytes 589832 | tf_op jit(solution)/shard_map/ppermute | solution.py:359
  164.3 31.7 %collective-permute-start.24 = (f32[3,128,128]{2,1,0:T(8,128)S(1)}, f32[3,128,128]{2,1,0:T(8,128)S(1)}, u32[]{:S(2)}, u32[]{:S(2)}) collective-permute-start(f32[3,128,128]{2,1,0:T(8,128)S(1)} %add.150), channel_id=1, source_target_pairs={{0,16},{4,20},{8,24},{12,28},{16,0},{20,4},{24,8},{28,12},{1,17},{... | collective-permute-start | bytes 589832 | tf_op jit(solution)/shard_map/ppermute | solution.py:359
  174.3 21.7 %collective-permute-start.23 = (f32[3,128,128]{2,1,0:T(8,128)S(1)}, f32[3,128,128]{2,1,0:T(8,128)S(1)}, u32[]{:S(2)}, u32[]{:S(2)}) collective-permute-start(f32[3,128,128]{2,1,0:T(8,128)S(1)} %add.150), channel_id=1, source_target_pairs={{0,8},{4,12},{8,0},{12,4},{16,24},{20,28},{24,16},{28,20},{1,9},{5... | collective-permute-start | bytes 589832 | tf_op jit(solution)/shard_map/ppermute | solution.py:359
  198.3 5.3 %collective-permute-start.18 = (f32[128,128]{1,0:T(8,128)S(1)}, f32[128,128]{1,0:T(8,128)S(1)}, u32[]{:S(2)}, u32[]{:S(2)}) collective-permute-start(f32[128,128]{1,0:T(8,128)S(1)} %add.143), channel_id=1, source_target_pairs={{0,24},{4,28},{8,16},{12,20},{16,8},{20,12},{24,0},{28,4},{1,25},{... | collective-permute-start | bytes 196616 | tf_op jit(solution)/shard_map/ppermute | solution.py:359
  202.5 8.2 %collective-permute-start.27 = (f32[2,128,128]{2,1,0:T(8,128)S(1)}, f32[2,128,128]{2,1,0:T(8,128)S(1)}, u32[]{:S(2)}, u32[]{:S(2)}) collective-permute-start(f32[2,128,128]{2,1,0:T(8,128)S(1)} %slice.49), channel_id=1, source_target_pairs={{0,2},{1,3},{2,0},{3,1},{4,6},{5,7},{6,4},{7,5},{8,10},{9,11},{10,... | collective-permute-start | bytes 393224 | tf_op jit(solution)/shard_map/ppermute | solution.py:365
  203.6 10.6 %collective-permute-start.28 = (f32[2,128,128]{2,1,0:T(8,128)S(1)}, f32[2,128,128]{2,1,0:T(8,128)S(1)}, u32[]{:S(2)}, u32[]{:S(2)}) collective-permute-start(f32[2,128,128]{2,1,0:T(8,128)S(1)} %slice.49), channel_id=1, source_target_pairs={{0,3},{1,0},{2,1},{3,2},{4,7},{5,4},{6,5},{7,6},{8,11},{9,8},{10,9... | collective-permute-start | bytes 393224 | tf_op jit(solution)/shard_map/ppermute | solution.py:365
  204.8 12.7 %collective-permute-start.26 = (f32[2,128,128]{2,1,0:T(8,128)S(1)}, f32[2,128,128]{2,1,0:T(8,128)S(1)}, u32[]{:S(2)}, u32[]{:S(2)}) collective-permute-start(f32[2,128,128]{2,1,0:T(8,128)S(1)} %slice.49), channel_id=1, source_target_pairs={{0,1},{1,2},{2,3},{3,0},{4,5},{5,6},{6,7},{7,4},{8,9},{9,10},{10,1... | collective-permute-start | bytes 393224 | tf_op jit(solution)/shard_map/ppermute | solution.py:365
  205.6 26.1 %collective-permute-start.21 = (f32[128,128]{1,0:T(8,128)S(1)}, f32[128,128]{1,0:T(8,128)S(1)}, u32[]{:S(2)}, u32[]{:S(2)}) collective-permute-start(f32[128,128]{1,0:T(8,128)S(1)} %add_add_fusion.3), channel_id=1, source_target_pairs={{0,3},{1,0},{2,1},{3,2},{4,7},{5,4},{6,5},{7,6},{8,11},{9,8},{10,9... | collective-permute-start | bytes 196616 | tf_op jit(solution)/shard_map/ppermute | solution.py:365
  210.7 21.1 %collective-permute-start.20 = (f32[128,128]{1,0:T(8,128)S(1)}, f32[128,128]{1,0:T(8,128)S(1)}, u32[]{:S(2)}, u32[]{:S(2)}) collective-permute-start(f32[128,128]{1,0:T(8,128)S(1)} %add_add_fusion.3), channel_id=1, source_target_pairs={{0,2},{1,3},{2,0},{3,1},{4,6},{5,7},{6,4},{7,5},{8,10},{9,11},{10,... | collective-permute-start | bytes 196616 | tf_op jit(solution)/shard_map/ppermute | solution.py:365
  214.2 17.5 %collective-permute-start.19 = (f32[128,128]{1,0:T(8,128)S(1)}, f32[128,128]{1,0:T(8,128)S(1)}, u32[]{:S(2)}, u32[]{:S(2)}) collective-permute-start(f32[128,128]{1,0:T(8,128)S(1)} %add_add_fusion.3), channel_id=1, source_target_pairs={{0,1},{1,2},{2,3},{3,0},{4,5},{5,6},{6,7},{7,4},{8,9},{9,10},{10,1... | collective-permute-start | bytes 196616 | tf_op jit(solution)/shard_map/ppermute | solution.py:365
  (21 other events, 168.0 us)
